TPU v7x, 256 devices: a whole 4x4x8 slice. The times are simulated.
256 devices in a mesh: ctx: 32 (over x_lo, z, core), head: 8 (over x_hi, y).
Axes of the slice: x: 4 (x_hi: 2, x_lo: 2; x = x_hi * 2 + x_lo), y: 4, z: 8, core: 2. Of those that a mesh axis runs over, the one named last changes fastest.
Arguments:
- tokens: bfloat16 [8192, 3072], P('ctx', 'head'), may hold values from -48 to 48
- block_order: int32 [64], replicated, may hold values from 0 to 63, each once
- block_mask: int32 [64, 64], replicated, may hold values from 0 to 1, as said below
- w_query: bfloat16 [3072, 3072], P(None, 'head'), may hold values from -0.109375 to 0.109375
- w_key: bfloat16 [3072, 3072], P(None, 'head'), may hold values from -0.109375 to 0.109375
- w_value: bfloat16 [3072, 3072], P(None, 'head'), may hold values from -0.109375 to 0.109375
- w_out: bfloat16 [3072, 3072], P('head'), may hold values from -0.109375 to 0.109375
Outputs:
- mixed: bfloat16 [8192, 3072], P('ctx', 'head')
Inputs may be any that keep to these rules, and one draw needn't show every extreme that they name: `block_order`: a permutation of the block numbers. block_mask[f, f] = 1 for every block f.
All inputs are finite; a program needn't handle non-finite values.
Results may differ from a plain program's by a relative error of at most 0.02.
The roundings to bfloat16 on the way count: a program that leaves them out, or rounds other values in their place, can miss the bound.
Values may be sent and summed in bfloat16 or wider, within the bound.
A program may use at most 128 MiB of HBM per device.

v0:
```python
import jax
import jax.numpy as jnp
from jax import lax
from jax.sharding import PartitionSpec as P

HEAD_DIM = 128
BLOCK = 128


def per_device(tokens, block_order, block_mask, w_query, w_key, w_value, w_out):
    row_count = tokens.shape[0]
    local_width = w_query.shape[1]
    local_heads = local_width // HEAD_DIM
    block_count = block_order.shape[0]
    portion = lax.all_gather(tokens, "head", axis=1, tiled=True)
    projected = tuple(
        (
            jnp.dot(portion, weight, preferred_element_type=jnp.float32)
            for weight in (w_query, w_key, w_value)
        )
    )
    query_rows, key_rows, value_rows = [
        part_sum.astype(jnp.bfloat16).reshape(row_count, local_heads, HEAD_DIM)
        for part_sum in projected
    ]
    frame_ids = jnp.arange(block_count, dtype=jnp.int32)
    placed = (block_order[None, :] == frame_ids[:, None]).astype(jnp.float32)
    mask_float = block_mask.astype(jnp.float32)
    cycle_live = jnp.dot(
        jnp.dot(placed.T, mask_float, precision=lax.Precision.HIGHEST),
        placed,
        precision=lax.Precision.HIGHEST,
    )
    cycle_index = lax.axis_index("ctx")
    global_rows = cycle_index * row_count + jnp.arange(row_count, dtype=jnp.int32)
    row_blocks = global_rows // BLOCK
    row_pick = (row_blocks[:, None] == frame_ids[None, :]).astype(jnp.float32)
    live_columns = jnp.dot(row_pick, cycle_live, precision=lax.Precision.HIGHEST).T
    inv_root = 1.0 / HEAD_DIM**0.5

    def update(state, key_tile, value_tile, key_keep):
        top_now, total_now, accum = state
        scores = (
            jnp.einsum("qhd,khd->hqk", query_rows, key_tile, preferred_element_type=jnp.float32)
            * inv_root
        )
        allowed = key_keep[None, :, None]
        top_next = jnp.maximum(top_now, jnp.max(jnp.where(allowed, scores, -1e30), axis=-1))
        factor = jnp.exp(top_now - top_next)
        weights = jnp.where(allowed, jnp.exp(scores - top_next[..., None]), 0.0)
        total_next = total_now * factor + jnp.sum(weights, axis=-1)
        accum = accum * factor[..., None] + jnp.einsum(
            "hqk,khd->hqd",
            weights.astype(jnp.bfloat16),
            value_tile,
            preferred_element_type=jnp.float32,
        )
        return (top_next, total_next, accum)

    initial = (
        jnp.full((local_heads, row_count), -1e30, jnp.float32),
        jnp.zeros((local_heads, row_count), jnp.float32),
        jnp.zeros((local_heads, row_count, HEAD_DIM), jnp.float32),
    )
    carry = initial
    key_part = lax.all_gather(key_rows, "ctx", axis=0, tiled=True)
    value_part = lax.all_gather(value_rows, "ctx", axis=0, tiled=True)
    tile_count = key_part.shape[0] // BLOCK
    key_tiles = key_part.reshape(tile_count, BLOCK, local_heads, HEAD_DIM)
    value_tiles = value_part.reshape(tile_count, BLOCK, local_heads, HEAD_DIM)

    def advance(state, inputs):
        key_tile, value_tile, offset = inputs
        key_keep = lax.dynamic_index_in_dim(live_columns, offset, 0, keepdims=False) > 0.5
        state = update(state, key_tile, value_tile, key_keep)
        return (state, None)

    carry, _ = lax.scan(
        advance, carry, (key_tiles, value_tiles, jnp.arange(tile_count, dtype=jnp.int32))
    )
    top_final, total_final, accum_final = carry
    attended = (
        (accum_final / total_final[..., None])
        .transpose(1, 0, 2)
        .reshape(row_count, local_width)
        .astype(jnp.bfloat16)
    )
    partial_out = jnp.dot(attended, w_out, preferred_element_type=jnp.float32)
    return lax.psum_scatter(
        partial_out.astype(jnp.bfloat16), "head", scatter_dimension=1, tiled=True
    )


def solution(mesh):
    in_specs = (
        P("ctx", "head"),
        P(),
        P(),
        P(None, "head"),
        P(None, "head"),
        P(None, "head"),
        P("head", None),
    )
    out_specs = P("ctx", "head")
    return jax.shard_map(
        per_device, mesh=mesh, in_specs=in_specs, out_specs=out_specs, check_vma=False
    )
```

profile of v0, /device:TPU:8, one launch (start us, length us, event | category | flops | bytes accessed | tf_op | source)
XLA Modules:
  0.0 651.9 jit_solution(12298507190897239615)
XLA Ops:
  7.3 58.7 %all-gather.4.cloned.1.call-done = bf16[256,3072]{1,0:T(8,128)(2,1)} async-done(((bf16[256,384]{1,0:T(8,128)(2,1)}), bf16[256,3072]{1,0:T(8,128)(2,1)}) %all-gather.4.cloned.1.call-update) | async-done | bytes 1572880 | tf_op jit(solution)/shard_map/all_gather | solution.py:15
  66.0 3.1 convolution_convert_fusion.1
  70.1 3.1 convolution_convert_fusion.3
  74.8 3.1 convolution_convert_fusion.2
  78.3 70.7 %all-gather.8.cloned.1.call-done = bf16[8192,3,128]{0,2,1:T(8,128)(2,1)} async-done(((bf16[256,3,128]{0,2,1:T(8,128)(2,1)}), bf16[8192,3,128]{0,2,1:T(8,128)(2,1)}) %all-gather.8.cloned.1.call-update) | async-done | bytes 6291472 | tf_op jit(solution)/shard_map/all_gather | solution.py:67
  149.0 8.6 %copy.25 = bf16[8192,3,128]{2,0,1:T(8,128)(2,1)} copy(bf16[8192,3,128]{0,2,1:T(8,128)(2,1)} %all-gather.8.cloned.1.call-done) | data formatting | bytes 12582912 | tf_op jit(solution)/shard_map/all_gather | solution.py:67
  157.6 71.3 %all-gather.6.cloned.1.call-done = bf16[8192,3,128]{0,2,1:T(8,128)(2,1)} async-done(((bf16[256,3,128]{0,2,1:T(8,128)(2,1)}), bf16[8192,3,128]{0,2,1:T(8,128)(2,1)}) %all-gather.6.cloned.1.call-update) | async-done | bytes 6291472 | tf_op jit(solution)/shard_map/all_gather | solution.py:66
  228.9 8.6 %copy.22 = bf16[8192,3,128]{2,0,1:T(8,128)(2,1)} copy(bf16[8192,3,128]{0,2,1:T(8,128)(2,1)} %all-gather.6.cloned.1.call-done) | data formatting | bytes 12582912 | tf_op jit(solution)/shard_map/all_gather | solution.py:66
  237.5 323.9 %while.15 = (s32[]{:T(128)}, f32[3,256]{1,0:T(4,128)S(1)}, f32[3,256]{1,0:T(4,128)S(1)}, f32[3,256,128]{2,1,0:T(8,128)S(1)}, s32[64]{0:T(128)S(1)}, /*index=5*/f...) while((s32[]{:T(128)}, f32[3,256]{1,0:T(4,128)S(1)}, ...), condition=%wide.region_3.4_spmd.clone, body=%wide.region_0.3_spmd.clone.sunk | while | flops 51515396 | bytes 2410691 | solution.py:78
  241.3 1.2 convolution_add_fusion.2
  246.4 1.2 convolution_add_fusion.2
  251.4 1.2 convolution_add_fusion.2
  256.5 1.2 convolution_add_fusion.2
  261.6 1.2 convolution_add_fusion.2
  266.6 1.2 convolution_add_fusion.2
  271.7 1.2 convolution_add_fusion.2
  276.8 1.2 convolution_add_fusion.2
  281.8 1.2 convolution_add_fusion.2
  286.9 1.2 convolution_add_fusion.2
  291.9 1.2 convolution_add_fusion.2
  297.0 1.2 convolution_add_fusion.2
  302.1 1.2 convolution_add_fusion.2
  307.1 1.2 convolution_add_fusion.2
  312.2 1.2 convolution_add_fusion.2
  317.2 1.2 convolution_add_fusion.2
  322.3 1.2 convolution_add_fusion.2
  327.4 1.2 convolution_add_fusion.2
  332.4 1.2 convolution_add_fusion.2
  337.5 1.2 convolution_add_fusion.2
  342.5 1.2 convolution_add_fusion.2
  347.6 1.2 convolution_add_fusion.2
  352.7 1.2 convolution_add_fusion.2
  357.7 1.2 convolution_add_fusion.2
  362.8 1.2 convolution_add_fusion.2
  367.8 1.2 convolution_add_fusion.2
  372.9 1.2 convolution_add_fusion.2
  378.0 1.2 convolution_add_fusion.2
  383.0 1.2 convolution_add_fusion.2
  393.2 1.2 convolution_add_fusion.2
  403.3 1.2 convolution_add_fusion.2
  408.3 1.2 convolution_add_fusion.2
  418.5 1.2 convolution_add_fusion.2
  423.5 1.2 convolution_add_fusion.2
  433.6 1.2 convolution_add_fusion.2
  438.7 1.2 convolution_add_fusion.2
  448.8 1.2 convolution_add_fusion.2
  458.9 1.2 convolution_add_fusion.2
  464.0 1.2 convolution_add_fusion.2
  474.1 1.2 convolution_add_fusion.2
  479.2 1.2 convolution_add_fusion.2
  489.3 1.2 convolution_add_fusion.2
  499.4 1.2 convolution_add_fusion.2
  504.5 1.2 convolution_add_fusion.2
  514.6 1.2 convolution_add_fusion.2
  519.7 1.2 convolution_add_fusion.2
  529.8 1.2 convolution_add_fusion.2
  534.9 1.2 convolution_add_fusion.2
  545.0 1.2 convolution_add_fusion.2
  555.1 1.2 convolution_add_fusion.2
  560.2 1.2 convolution_add_fusion.2
  561.6 2.2 convolution_convert_fusion
  563.8 2.6 copy.31
  566.4 77.2 %reduce-scatter.4.cloned.1.call-done = bf16[384,256]{1,0:T(8,128)(2,1)} async-done(((bf16[3072,256]{1,0:T(8,128)(2,1)}), bf16[384,256]{1,0:T(8,128)(2,1)}) %reduce-scatter.4.cloned.1.call-update) | async-done | bytes 196624
  643.6 1.7 copy.32
  (489 shorter events, 138.4 us)
Async XLA Ops:
  6.5 555.1 %copy-start = (bf16[384,3072]{1,0:T(8,128)(2,1)S(1)}, bf16[384,3072]{1,0:T(8,128)(2,1)}, u32[]{:S(2)}) copy-start(bf16[384,3072]{1,0:T(8,128)(2,1)} %param.15) | copy-start | bytes 7077892
  6.5 59.5 %all-gather.4.cloned.1.call-start = ((), (), s32[]{:S(2)}) async-start(), calls=%async_computation.1 | async-start | bytes 1769472 | tf_op jit(solution)/shard_map/all_gather | solution.py:15
  7.3 141.8 %all-gather.8.cloned.1.call-start = ((), (), s32[]{:S(2)}) async-start(), calls=%async_computation.3 | async-start | bytes 6488064 | tf_op jit(solution)/shard_map/all_gather | solution.py:67
  70.0 4.2 copy-start.1
  70.0 4.2 copy-start.2
  70.0 158.9 %all-gather.6.cloned.1.call-start = ((), (), s32[]{:S(2)}) async-start(), calls=%async_computation.2 | async-start | bytes 6488064 | tf_op jit(solution)/shard_map/all_gather | solution.py:66
  74.0 569.6 %reduce-scatter.4.cloned.1.call-start = ((), (), s32[]{:S(2)}) async-start(), calls=%async_computation.4 | async-start | bytes 1769472
Sparse Core Ops, SparseCore 0:
  9.8 56.1 all-gather.3
  70.1 78.8 all-gather.7
  150.8 78.0 all-gather.5
  566.5 77.0 reduce-scatter.3
where the time goes:
time: 658 us; the launch traced here: 652 us
  waiting for transfers between devices  279 us (42%)
  matrix products  162 us (25%)
  loops' own time  127 us (19%)
  local copies, waits for them, and re-layouts  61.4 us (9%)
  between operations  13.3 us (2%)
  other arithmetic  8.91 us (1%)
    another operation x1, loops' own time, per_device(): lax.scan(advance, carry, (key_tiles, value_tiles, jnp.arange(tile_count,...  127 us
    unnamed x5, waiting for transfers between devices  78 us
    dot_general x64, matrix products, update(): jnp.einsum('hqk,khd->hqd', weights.astype(jnp.bfloat16), value_tile, pref...  77.5 us
    dot_general x64, matrix products, update(): jnp.einsum('qhd,khd->hqk', query_rows, key_tile, preferred_element_type=j...  72.4 us
    all_gather x1, waiting for transfers between devices, per_device(): key_part = lax.all_gather(key_rows, 'ctx', axis=0, tiled=True)  71.3 us
    all_gather x1, waiting for transfers between devices, per_device(): value_part = lax.all_gather(value_rows, 'ctx', axis=0, tiled=True)  70.7 us
    all_gather x1, waiting for transfers between devices, per_device(): portion = lax.all_gather(tokens, 'head', axis=1, tiled=True)  58.7 us
    dynamic_slice x64, local copies, waits for them, and re-layouts, per_device(): lax.scan(advance, carry, (key_tiles, value_tiles, jnp.arange(tile_count,...  37.5 us
  transfers between devices with their start and end apart: 4, of which 4 were waited for; matrix products, arithmetic and copies ran while one was open for 3% of the time, Pallas kernels for 0%

commit v1 on v0

v1 whole, which is shorter than its diff:
```python
import functools

import jax
import jax.numpy as jnp
from jax import lax
from jax.experimental import pallas as pl
from jax.experimental.pallas import tpu as pltpu
from jax.sharding import PartitionSpec as P

MESH = pl.DeviceIdType.MESH
HD = 128
BLK = 128
HEADS = 3
ROWS = 256
COLS = 384
NX, NY, NZ = 4, 4, 8
UNITS = 2 * HEADS
DEPTH = 3
NEG = -1e30
SCALE2 = 1.4426950408889634 / HD**0.5


def kernel(
    order_ref, mask_ref, tok_in, wq_hbm, wk_hbm, wv_hbm, wo_hbm, out_ref,
    tok, wbuf, wo, acc, qall, kv, m_s, l_s, o_s, osend, ssend, orecv, srecv, asend, att, out_acc,
    w_sem, xs, xr, ys, yr, zs, zr, qs, qr, os_, or_, ss_, sr_, axs, axr, ays, ayr, ws, wr, ps, pr,
):
    ctx = lax.axis_index("ctx")
    hd = lax.axis_index("head")
    x_lo, z, c = ctx // 16, (ctx // 2) % 8, ctx % 2
    x_hi, y = hd // 4, hd % 4
    x = 2 * x_hi + x_lo

    def dev(xx, yy, zz, cc):
        return ((xx % 2) * 16 + zz * 2 + cc, (xx // 2) * 4 + yy)

    xp, xm = (x + 1) % NX, (x + NX - 1) % NX
    yp, ym, y2 = (y + 1) % NY, (y + NY - 1) % NY, (y + 2) % NY
    zp, zm = (z + 1) % NZ, (z + NZ - 1) % NZ
    xn = x_hi * 2 + (1 - x_lo)
    xc = NX - 1 - x
    pc = 1 - c
    d_xp, d_xm = dev(xp, y, z, c), dev(xm, y, z, c)
    d_yp, d_ym = dev(x, yp, z, c), dev(x, ym, z, c)
    d_zp, d_zm = dev(x, y, zp, c), dev(x, y, zm, c)
    sibs = (dev(x, y, z, pc), dev(xn, y, z, c), dev(xn, y, z, pc))
    sib_slot = (x_lo * 2 + pc, (1 - x_lo) * 2 + c, (1 - x_lo) * 2 + pc)
    me_slot = x_lo * 2 + c
    wpeers = [
        (x_hi * 4 + yp, dev(x, yp, z, c), 0), (x_hi * 4 + ym, dev(x, ym, z, c), 1),
        (x_hi * 4 + y2, dev(x, y2, z, c), 2), ((1 - x_hi) * 4 + y, dev(xc, y, z, c), 3),
        ((1 - x_hi) * 4 + yp, dev(xc, yp, z, c), 4), ((1 - x_hi) * 4 + ym, dev(xc, ym, z, c), 5),
        ((1 - x_hi) * 4 + y2, dev(xc, y2, z, c), 6),
    ]
    back = (1, 0, 2, 3, 5, 4, 6)

    started = []

    def send(src, dst, s_sem, r_sem, to):
        copy = pltpu.make_async_remote_copy(
            src_ref=src, dst_ref=dst, send_sem=s_sem, recv_sem=r_sem,
            device_id=to, device_id_type=MESH,
        )
        copy.start()
        started.append(copy)

    def arrived(ref, s_sem, r_sem):
        pltpu.make_async_remote_copy(
            src_ref=ref, dst_ref=ref, send_sem=s_sem, recv_sem=r_sem,
            device_id=d_zp, device_id_type=MESH,
        ).wait_recv()

    loads = [
        pltpu.make_async_copy(w, wbuf.at[i], w_sem.at[i])
        for i, w in enumerate((wk_hbm, wv_hbm, wq_hbm))
    ]
    for load in loads:
        load.start()
    own_out = pltpu.make_async_copy(
        wo_hbm.at[:, pl.ds(pl.multiple_of(hd * COLS, COLS), COLS)], wo.at[hd], w_sem.at[3]
    )
    own_out.start()

    barrier = pltpu.get_barrier_semaphore()
    peers = [d_xp, d_xm, d_yp, d_ym, d_zp, d_zm, sibs[0], sibs[2]]
    peers += [wpeers[2][1], wpeers[4][1], wpeers[5][1], wpeers[6][1]]
    for peer in peers:
        pl.semaphore_signal(barrier, inc=1, device_id=peer, device_id_type=MESH)
    pl.semaphore_wait(barrier, len(peers))

    send(tok_in, tok.at[hd], xs.at[0], xr.at[0], d_xp)
    send(tok_in, tok.at[hd], xs.at[1], xr.at[1], d_xm)

    def x_arrived(buf, r_sem, s_sem):
        arrived(buf.at[(xm // 2) * 4 + y], s_sem.at[0], r_sem.at[0])
        arrived(buf.at[(xp // 2) * 4 + y], s_sem.at[1], r_sem.at[1])

    def y_first(buf, s_sem, r_sem):
        send(buf.at[y], buf.at[y], s_sem.at[0], r_sem.at[0], d_yp)
        send(buf.at[4 + y], buf.at[4 + y], s_sem.at[1], r_sem.at[1], d_ym)
        send(buf.at[4 + y], buf.at[4 + y], s_sem.at[2], r_sem.at[2], d_yp)
        send(buf.at[y], buf.at[y], s_sem.at[3], r_sem.at[3], d_ym)

    def y_second(buf, s_sem, r_sem):
        arrived(buf.at[ym], s_sem.at[0], r_sem.at[0])
        send(buf.at[ym], buf.at[ym], s_sem.at[4], r_sem.at[4], d_yp)
        arrived(buf.at[4 + yp], s_sem.at[1], r_sem.at[1])
        send(buf.at[4 + yp], buf.at[4 + yp], s_sem.at[5], r_sem.at[5], d_ym)
        arrived(buf.at[4 + ym], s_sem.at[2], r_sem.at[2])
        arrived(buf.at[yp], s_sem.at[3], r_sem.at[3])

    def y_last(buf, s_sem, r_sem):
        arrived(buf.at[y2], s_sem.at[4], r_sem.at[4])
        arrived(buf.at[4 + y2], s_sem.at[5], r_sem.at[5])

    def project(yy, first):
        for shard in range(2):
            g = shard * 4 + yy

            def one(w, carry, g=g, init=first and shard == 0):
                part = jnp.dot(
                    tok[g], wbuf[w, pl.ds(pl.multiple_of(g * COLS, COLS), COLS), :],
                    preferred_element_type=jnp.float32,
                )
                if init:
                    acc[w] = part
                else:
                    acc[w] = acc[w] + part
                return carry

            lax.fori_loop(0, 3, one, 0)

    x_arrived(tok, xr, xs)
    y_first(tok, ys, yr)
    for load in loads:
        load.wait()
    project(y, True)
    y_second(tok, ys, yr)
    project(ym, False)
    project(yp, False)
    y_last(tok, ys, yr)
    project(y2, False)

    for h in range(HEADS):
        cols = slice(h * HD, (h + 1) * HD)
        kv[z, h, :, 0:HD] = acc[0, :, cols].astype(jnp.bfloat16)
        kv[z, h, :, HD : 2 * HD] = acc[1, :, cols].astype(jnp.bfloat16)
        qall[me_slot, h] = acc[2, :, cols].astype(jnp.bfloat16)

    def piece(zz, u):
        return kv.at[zz, u // 2, pl.ds((u % 2) * BLK, BLK), :]

    def z_send(direction, s, u):
        if s == 4 and direction != u % 2:
            return
        if direction == 0:
            ref, to = piece((z + NZ - (s - 1)) % NZ, u), d_zp
        else:
            ref, to = piece((z + (s - 1)) % NZ, u), d_zm
        send(ref, ref, zs.at[direction, s - 1, u], zr.at[direction, s - 1, u], to)

    def z_arrived(direction, s, u):
        if s == 4 and direction != u % 2:
            return
        src = (z + NZ - s) % NZ if direction == 0 else (z + s) % NZ
        arrived(piece(src, u), zs.at[direction, s - 1, u], zr.at[direction, s - 1, u])

    for u in range(DEPTH):
        z_send(0, 1, u)
        z_send(1, 1, u)
    for i in (1, 2, 0):
        send(qall.at[me_slot], qall.at[me_slot], qs.at[i], qr.at[i], sibs[i])
    half = COLS // 2
    my_half = pl.ds(pl.multiple_of(c * half, half), half)
    other_half = pl.ds(pl.multiple_of(pc * half, half), half)
    for g, to, i in wpeers:
        send(
            wo_hbm.at[my_half, pl.ds(pl.multiple_of(g * COLS, COLS), COLS)],
            wo.at[hd, my_half, :], ws.at[i], wr.at[i], to,
        )

    def relay_out_weights():
        for g, _, i in wpeers:
            arrived(wo.at[g, my_half, :], ws.at[back[i]], wr.at[back[i]])
            send(wo.at[g, my_half, :], wo.at[g, my_half, :], ps.at[i], pr.at[i], sibs[0])

    def out_weights_arrived():
        own_out.wait()
        for g, _, i in wpeers:
            arrived(wo.at[g, other_half, :], ps.at[i], pr.at[i])

    def bias_of(q_slot, qi, src, r):
        q_ctx = (1 - q_slot // 2) * 16 + z * 2 + q_slot % 2
        k_ctx = (1 - x_lo) * 16 + src * 2 + c
        live = mask_ref[order_ref[2 * q_ctx + qi], order_ref[2 * k_ctx + r]]
        return jnp.where(live > 0, 0.0, NEG).astype(jnp.float32)

    def attend(h, s):
        if s == 0:
            srcs = [z]
        elif s == 4:
            srcs = [(z + 4) % NZ]
        else:
            srcs = [(z + NZ - s) % NZ, (z + s) % NZ]

        def body(slot, carry):
            q = qall[slot, h]
            scores = []
            for src in srcs:
                raw = lax.dot_general(
                    q, kv[src, h, :, 0:HD], (((1,), (1,)), ((), ())),
                    preferred_element_type=jnp.float32,
                )
                for r in range(2):
                    block = raw[:, r * BLK : (r + 1) * BLK]
                    scores.append(
                        jnp.concatenate(
                            [
                                block[qi * BLK : (qi + 1) * BLK] * SCALE2 + bias_of(slot, qi, src, r)
                                for qi in range(2)
                            ],
                            axis=0,
                        )
                    )
            top = functools.reduce(jnp.maximum, scores)
            top = jnp.broadcast_to(jnp.max(top, axis=1, keepdims=True), (ROWS, HD))
            if s > 0:
                before = m_s[h, slot]
                top = jnp.maximum(before, top)
                factor = jnp.exp2(before - top)
            weights = [jnp.exp2(score - top) for score in scores]
            total = functools.reduce(jnp.add, weights)
            mixed = None
            for i, src in enumerate(srcs):
                rounded = jnp.concatenate(
                    [weights[2 * i].astype(jnp.bfloat16), weights[2 * i + 1].astype(jnp.bfloat16)],
                    axis=1,
                )
                part = jnp.dot(
                    rounded, kv[src, h, :, HD : 2 * HD], preferred_element_type=jnp.float32
                )
                mixed = part if mixed is None else mixed + part
            if s > 0:
                total = total + l_s[h, slot] * factor
                mixed = mixed + o_s[h, slot] * factor
            m_s[h, slot] = top
            l_s[h, slot] = total
            o_s[h, slot] = mixed
            return carry

        lax.fori_loop(0, 4, body, 0)

    def share(h):
        for i in range(3):
            slot = sib_slot[i]
            osend[h, i] = o_s[h, slot].astype(jnp.bfloat16)
            total = jnp.broadcast_to(
                jnp.sum(l_s[h, slot], axis=1, keepdims=True), (ROWS, HD)
            )
            ssend[h, i, 0:8, :] = jnp.transpose(m_s[h, slot])[0:8]
            ssend[h, i, 8:16, :] = jnp.transpose(total)[0:8]
        for i in (1, 2, 0):
            send(ssend.at[h, i], srecv.at[h, i], ss_.at[h, i], sr_.at[h, i], sibs[i])
            send(osend.at[h, i], orecv.at[h, i], os_.at[h, i], or_.at[h, i], sibs[i])

    def combine(h):
        tops = [m_s[h, me_slot]]
        totals = [
            jnp.broadcast_to(jnp.sum(l_s[h, me_slot], axis=1, keepdims=True), (ROWS, HD))
        ]
        parts = [o_s[h, me_slot]]
        for i in range(3):
            arrived(srecv.at[h, i], ss_.at[h, i], sr_.at[h, i])
            arrived(orecv.at[h, i], os_.at[h, i], or_.at[h, i])
            tops.append(jnp.transpose(jnp.broadcast_to(srecv[h, i, 0:1, :], (HD, ROWS))))
            totals.append(jnp.transpose(jnp.broadcast_to(srecv[h, i, 8:9, :], (HD, ROWS))))
            parts.append(orecv[h, i].astype(jnp.float32))
        top = functools.reduce(jnp.maximum, tops)
        scale = [jnp.exp2(t - top) for t in tops]
        total = functools.reduce(jnp.add, [a * b for a, b in zip(scale, totals)])
        mixed = functools.reduce(jnp.add, [a * b for a, b in zip(scale, parts)])
        asend[h] = (mixed / total).astype(jnp.bfloat16)
        send(asend.at[h], att.at[h, hd], axs.at[h, 0], axr.at[h, 0], d_xp)
        send(asend.at[h], att.at[h, hd], axs.at[h, 1], axr.at[h, 1], d_xm)

    def out_part(h, yy, first):
        for hi in range(2):
            g = hi * 4 + yy
            part = jnp.dot(
                att[h, g], wo[g, h * HD : (h + 1) * HD, :], preferred_element_type=jnp.float32
            )
            if first and hi == 0:
                out_acc[...] = part
            else:
                out_acc[...] = out_acc[...] + part

    def att_first(h):
        x_arrived(att.at[h], axr.at[h], axs.at[h])
        y_first(att.at[h], ays.at[h], ayr.at[h])

    def att_second(h):
        y_second(att.at[h], ays.at[h], ayr.at[h])

    def att_last(h):
        if h == 0:
            out_weights_arrived()
        out_part(h, y, h == 0)
        out_part(h, ym, False)
        out_part(h, yp, False)
        y_last(att.at[h], ays.at[h], ayr.at[h])
        out_part(h, y2, False)

    for k in range(0, UNITS + 4 + 5):
        for s in (4, 3, 2, 1):
            u = k - s
            if 0 <= u < UNITS:
                for direction in range(2):
                    z_arrived(direction, s, u)
                    if s < 4:
                        z_send(direction, s + 1, u)
        if DEPTH <= k + DEPTH < UNITS:
            z_send(0, 1, k + DEPTH)
            z_send(1, 1, k + DEPTH)
        if k == 5:
            relay_out_weights()
        for h in range(HEADS):
            done = 2 * h + 5
            if k == done + 1:
                combine(h)
            if k == done + 2:
                att_first(h)
            if k == done + 3:
                att_second(h)
            if k == done + 4:
                att_last(h)
        if k == 1:
            for i in range(3):
                arrived(qall.at[sib_slot[i]], qs.at[i], qr.at[i])
        for h in range(HEADS):
            s = k - (2 * h + 1)
            if 0 <= s <= 4:
                attend(h, s)
                if s == 4:
                    share(h)

    out_ref[...] = out_acc[...].astype(jnp.bfloat16)
    for copy in started:
        copy.wait_send()


def per_device(tokens, block_order, block_mask, w_query, w_key, w_value, w_out):
    bf, f32 = jnp.bfloat16, jnp.float32
    sem = pltpu.SemaphoreType.DMA
    smem = pl.BlockSpec(memory_space=pltpu.SMEM)
    vmem = pl.BlockSpec(memory_space=pltpu.VMEM)
    anywhere = pl.BlockSpec(memory_space=pl.ANY)
    return pl.pallas_call(
        kernel,
        out_shape=jax.ShapeDtypeStruct((ROWS, COLS), bf),
        in_specs=[smem, smem, vmem, anywhere, anywhere, anywhere, anywhere],
        out_specs=vmem,
        scratch_shapes=[
            pltpu.VMEM((8, ROWS, COLS), bf),
            pltpu.VMEM((3, 3072, COLS), bf),
            pltpu.VMEM((8, COLS, COLS), bf),
            pltpu.VMEM((3, ROWS, COLS), f32),
            pltpu.VMEM((4, HEADS, ROWS, HD), bf),
            pltpu.VMEM((NZ, HEADS, ROWS, 2 * HD), bf),
            pltpu.VMEM((HEADS, 4, ROWS, HD), f32),
            pltpu.VMEM((HEADS, 4, ROWS, HD), f32),
            pltpu.VMEM((HEADS, 4, ROWS, HD), f32),
            pltpu.VMEM((HEADS, 3, ROWS, HD), bf),
            pltpu.VMEM((HEADS, 3, 16, ROWS), f32),
            pltpu.VMEM((HEADS, 3, ROWS, HD), bf),
            pltpu.VMEM((HEADS, 3, 16, ROWS), f32),
            pltpu.VMEM((HEADS, ROWS, HD), bf),
            pltpu.VMEM((HEADS, 8, ROWS, HD), bf),
            pltpu.VMEM((ROWS, COLS), f32),
            sem((4,)),
            sem((2,)), sem((2,)),
            sem((6,)), sem((6,)),
            sem((2, 4, UNITS)), sem((2, 4, UNITS)),
            sem((3,)), sem((3,)),
            sem((HEADS, 3)), sem((HEADS, 3)),
            sem((HEADS, 3)), sem((HEADS, 3)),
            sem((HEADS, 2)), sem((HEADS, 2)),
            sem((HEADS, 6)), sem((HEADS, 6)),
            sem((7,)), sem((7,)),
            sem((7,)), sem((7,)),
        ],
        compiler_params=pltpu.CompilerParams(
            collective_id=0, has_side_effects=True, vmem_limit_bytes=60 * 1024 * 1024
        ),
    )(block_order, block_mask, tokens, w_query, w_key, w_value, w_out)


def solution(mesh):
    in_specs = (
        P("ctx", "head"),
        P(),
        P(),
        P(None, "head"),
        P(None, "head"),
        P(None, "head"),
        P("head", None),
    )
    return jax.shard_map(
        per_device, mesh=mesh, in_specs=in_specs, out_specs=P("ctx", "head"), check_vma=False
    )
```

time: 658 us -> 103 us (0.16)
  waiting for transfers between devices: 279 us -> 0 us
  matrix products: 162 us -> 0 us
  loops' own time: 127 us -> 0 us
  Pallas kernels: 0 us -> 102 us
  local copies, waits for them, and re-layouts: 61.4 us -> 1.62 us
  between operations: 13.3 us -> 0.01 us
  other arithmetic: 8.91 us -> 0 us
    all_gather x3 -> x0, waiting for transfers between devices: 201 us -> none  [the longest x1 71.3 us: per_device(): key_part = lax.all_gather(key_rows, 'ctx', axis=0, tiled=True)]
    dot_general x135 -> x0, matrix products: 162 us -> none  [the longest x64 77.5 us: update(): jnp.einsum('hqk,khd->hqd', weights.astype(jnp.bfloat16), value_tile, pref...]
    another operation x1 -> x0, loops' own time: 127 us -> none  [per_device(): lax.scan(advance, carry, (key_tiles, value_tiles, jnp.arange(tile_count,...]
    pallas_call x0 -> x1, Pallas kernels: none -> 102 us  [per_device(): pl.pallas_call(kernel, out_shape=jax.ShapeDtypeStruct((ROWS, COLS), bf),...]
    unnamed x5 -> x0, waiting for transfers between devices: 78 us -> none
    dynamic_slice x64 -> x0, local copies, waits for them, and re-layouts: 37.5 us -> none  [per_device(): lax.scan(advance, carry, (key_tiles, value_tiles, jnp.arange(tile_count,...]
    all_gather x2 -> x0, local copies, waits for them, and re-layouts: 17.2 us -> none  [the longest x1 8.61 us: per_device(): value_part = lax.all_gather(value_rows, 'ctx', axis=0, tiled=True)]
  transfers between devices with their start and end apart: 4 -> 0, of which waited for: 4 -> 0; matrix products, arithmetic and copies ran while one was open for 3% -> 0% of each run, Pallas kernels for 0% -> 0%
where the time goes in v1:
time: 103 us
  Pallas kernels  102 us (99%)
  local copies, waits for them, and re-layouts  1.62 us (2%)
    pallas_call x1, Pallas kernels, per_device(): pl.pallas_call(kernel, out_shape=jax.ShapeDtypeStruct((ROWS, COLS), bf),...  102 us

profile of v1, /device:TPU:8, one launch (start us, length us, event | category | flops | bytes accessed | tf_op | source)
XLA Modules:
  0.0 103.2 jit_solution(3941118618912930788)
XLA Ops:
  0.0 101.5 %shard_map.73 = bf16[256,384]{1,0:T(8,128)(2,1)} custom-call(s32[64]{0:T(128)} %order_ref.1, s32[64,64]{1,0:T(8,128)} %mask_ref.1, bf16[256,384]{1,0:T(8,128)(2,1)} %tok_in.1, bf16[3072,384]{1,0:T(8,128)(2,1)} %wq_hbm.1, bf16[3072,384]{1,0:T(8,128)(2,1)} %wk_hbm.1, bf16[3072,384]{1,0:T(8,128)(2,1)} %wv_hbm.1, bf16[384,3072]{1,0:T(8,128)(2,1)} %wo_hbm.1), custom_call_target="tpu_custom_call" | custom-call | tf_op jit(solution)/shard_map/pallas_call | solution.py:357
  101.6 1.6 %copy.9 = bf16[256,384]{1,0:T(8,128)(2,1)} copy(bf16[256,384]{1,0:T(8,128)(2,1)} %shard_map.73) | data formatting | bytes 393216

commit v2 on v0

v2 whole, which is shorter than its diff:
```python
import functools

import jax
import jax.numpy as jnp
from jax import lax
from jax.experimental import pallas as pl
from jax.experimental.pallas import tpu as pltpu
from jax.sharding import PartitionSpec as P

MESH = pl.DeviceIdType.MESH
HD = 128
BLK = 128
HEADS = 3
ROWS = 256
HALF = 128
COLS = 384
NX, NY, NZ = 4, 4, 8
NEG = -1e30
LOW = -1e20
SCALE2 = 1.4426950408889634 / HD**0.5


START = ((0, 0, 0), (2, 3, 4))
GROUPS = (((0, 1), (1, 1), (1, -1), (2, 1)), ((2, -1), (3, 1), (3, -1), (4, 1)))


def kernel(
    order_ref, mask_ref, tok_in, wq_hbm, wk_hbm, wv_hbm, wo_hbm, out_ref,
    tok, wbuf, wo, acc, qall, kv, m_s, l_s, o_s, o1, s1, o1r, s1r, o2, s2, o2r, s2r, asend, att, out_acc,
    w_sem, xs, xr, ys, yr, zs, zr, qs, qr, cs, cr, as_, axr, ayr, ws, wr,
):
    ctx = lax.axis_index("ctx")
    hd = lax.axis_index("head")
    x_lo, z, c = ctx // 16, (ctx // 2) % 8, ctx % 2
    x_hi, y = hd // 4, hd % 4
    x = 2 * x_hi + x_lo

    def dev(xx, yy, zz, cc):
        return ((xx % 2) * 16 + zz * 2 + cc, (xx // 2) * 4 + yy)

    xp, xm = (x + 1) % NX, (x + NX - 1) % NX
    yp, ym, y2 = (y + 1) % NY, (y + NY - 1) % NY, (y + 2) % NY
    zp, zm = (z + 1) % NZ, (z + NZ - 1) % NZ
    x_far = 1 - x_lo
    xc = NX - 1 - x
    pc = 1 - c
    d_xp, d_xm = dev(xp, y, z, c), dev(xm, y, z, c)
    d_yp, d_ym = dev(x, yp, z, c), dev(x, ym, z, c)
    d_zp, d_zm = dev(x, y, zp, c), dev(x, y, zm, c)
    d_core = dev(x, y, z, pc)
    d_far = dev(x_hi * 2 + x_far, y, z, c)
    wpeers = [
        (x_hi * 4 + yp, dev(x, yp, z, c)), (x_hi * 4 + ym, dev(x, ym, z, c)),
        (x_hi * 4 + y2, dev(x, y2, z, c)), ((1 - x_hi) * 4 + y, dev(xc, y, z, c)),
        ((1 - x_hi) * 4 + yp, dev(xc, yp, z, c)), ((1 - x_hi) * 4 + ym, dev(xc, ym, z, c)),
        ((1 - x_hi) * 4 + y2, dev(xc, y2, z, c)),
    ]

    def send(src, dst, s_sem, r_sem, to):
        pltpu.make_async_remote_copy(
            src_ref=src, dst_ref=dst, send_sem=s_sem, recv_sem=r_sem,
            device_id=to, device_id_type=MESH,
        ).start()

    def arrived(ref, r_sem):
        pltpu.make_async_remote_copy(
            src_ref=ref, dst_ref=ref, send_sem=zs, recv_sem=r_sem,
            device_id=d_zp, device_id_type=MESH,
        ).wait_recv()

    def sent(ref, s_sem):
        pltpu.make_async_remote_copy(
            src_ref=ref, dst_ref=ref, send_sem=s_sem, recv_sem=wr.at[0],
            device_id=d_zp, device_id_type=MESH,
        ).wait_send()

    loads = [
        pltpu.make_async_copy(w, wbuf.at[i], w_sem.at[i])
        for i, w in enumerate((wk_hbm, wv_hbm, wq_hbm))
    ]
    for load in loads:
        load.start()
    own_out = pltpu.make_async_copy(
        wo_hbm.at[:, pl.ds(pl.multiple_of(hd * COLS, COLS), COLS)], wo.at[hd], w_sem.at[3]
    )
    own_out.start()

    barrier = pltpu.get_barrier_semaphore()
    peers = [d_xp, d_xm, d_yp, d_ym, d_zp, d_zm, d_core]
    peers += [wpeers[i][1] for i in (2, 4, 5, 6)]
    for peer in peers:
        pl.semaphore_signal(barrier, inc=1, device_id=peer, device_id_type=MESH)
    pl.semaphore_wait(barrier, len(peers))

    def x_arrived(at, r_sem):
        arrived(at((xm // 2) * 4 + y), r_sem.at[0])
        arrived(at((xp // 2) * 4 + y), r_sem.at[1])

    def y_first(at, s_sem, r_sem):
        send(at(y), at(y), s_sem, r_sem.at[0], d_yp)
        send(at(4 + y), at(4 + y), s_sem, r_sem.at[1], d_ym)
        send(at(4 + y), at(4 + y), s_sem, r_sem.at[2], d_yp)
        send(at(y), at(y), s_sem, r_sem.at[3], d_ym)

    def y_second(at, s_sem, r_sem):
        arrived(at(ym), r_sem.at[0])
        send(at(ym), at(ym), s_sem, r_sem.at[4], d_yp)
        arrived(at(4 + yp), r_sem.at[1])
        send(at(4 + yp), at(4 + yp), s_sem, r_sem.at[5], d_ym)
        arrived(at(4 + ym), r_sem.at[2])
        arrived(at(yp), r_sem.at[3])

    def y_last(at, r_sem):
        arrived(at(y2), r_sem.at[4])
        arrived(at(4 + y2), r_sem.at[5])

    def tok_at(r):
        return lambda g: tok.at[r, g]

    def att_at(h):
        return lambda g: att.at[h, g]

    def rows_of(g):
        return pl.ds(pl.multiple_of(g * COLS, COLS), COLS)

    def product(r, yy, h):
        left = jnp.concatenate([tok[r, yy], tok[r, 4 + yy]], axis=1)
        cols = pl.ds(pl.multiple_of(h * HD, HD), HD)
        right = jnp.concatenate(
            [
                jnp.concatenate([wbuf[i, rows_of(g), cols] for i in range(3)], axis=1)
                for g in (yy, 4 + yy)
            ],
            axis=0,
        )
        return jnp.dot(left, right, preferred_element_type=jnp.float32)

    def project(r, yy, first=False):
        def one(h, carry):
            part = product(r, yy, h)
            acc[r, h] = part if first else acc[r, h] + part
            return carry

        lax.fori_loop(0, HEADS, one, 0)

    def z_send(direction, s, h, r):
        if s == 4 and direction != r:
            return
        if direction == 0:
            ref, to = kv.at[(z + NZ - (s - 1)) % NZ, h, r], d_zp
        else:
            ref, to = kv.at[(z + (s - 1)) % NZ, h, r], d_zm
        send(ref, ref, zs, zr.at[direction, s - 1, h, r], to)

    def z_arrived(direction, s, h, r):
        if s == 4 and direction != r:
            return
        src = (z + NZ - s) % NZ if direction == 0 else (z + s) % NZ
        arrived(kv.at[src, h, r], zr.at[direction, s - 1, h, r])

    def z_start(h, r):
        z_send(0, 1, h, r)
        z_send(1, 1, h, r)

    def z_round(k):
        for s in (4, 3, 2, 1):
            for r in range(2):
                for h in range(HEADS):
                    if k == START[r][h] + s:
                        for direction in range(2):
                            z_arrived(direction, s, h, r)
                            if s < 4:
                                z_send(direction, s + 1, h, r)
        for h in range(HEADS):
            if k == START[1][h] and k > START[1][0]:
                z_start(h, 1)

    me_slot, core_slot = x_lo * 2 + c, x_lo * 2 + pc
    far_slot, far_core_slot = x_far * 2 + c, x_far * 2 + pc

    def finish(r):
        for h in range(HEADS):
            rows = acc[r, h] + product(r, y2, h)
            kv[z, h, r, 0] = rows[:, 0:HD].astype(jnp.bfloat16)
            kv[z, h, r, 1] = jnp.transpose(rows[:, HD : 2 * HD]).astype(jnp.bfloat16)
            qall[me_slot, r, h] = rows[:, 2 * HD :].astype(jnp.bfloat16)
            if START[r][h] == START[r][0]:
                z_start(h, r)
        mine = qall.at[me_slot, r]
        send(mine, mine, qs, qr.at[r, 0], d_far)
        send(mine, mine, qs, qr.at[r, 1], d_core)

    def q_relay(r):
        theirs = qall.at[far_slot, r]
        arrived(theirs, qr.at[r, 0])
        send(theirs, theirs, qs, qr.at[r, 2], d_core)

    def q_arrived():
        for r in range(2):
            arrived(qall.at[core_slot, r], qr.at[r, 1])
            arrived(qall.at[far_core_slot, r], qr.at[r, 2])

    half = COLS // 2
    my_half = pl.ds(pl.multiple_of(c * half, half), half)
    other_half = pl.ds(pl.multiple_of(pc * half, half), half)

    def out_weights():
        for i, (g, to) in enumerate(wpeers):
            send(
                wo_hbm.at[my_half, pl.ds(pl.multiple_of(g * COLS, COLS), COLS)],
                wo.at[hd, my_half, :], ws, wr.at[i], to,
            )

    def out_weights_relay():
        for i, j in enumerate((1, 0, 2, 3, 5, 4, 6)):
            piece = wo.at[wpeers[i][0], my_half, :]
            arrived(piece, wr.at[j])
            send(piece, piece, ws, wr.at[7 + i], d_core)

    def out_weights_arrived():
        own_out.wait()
        for i in range(7):
            arrived(wo.at[wpeers[i][0], other_half, :], wr.at[7 + i])

    def bias_row(q_slot, src, r):
        q_ctx = (1 - q_slot // 2) * 16 + z * 2 + q_slot % 2
        k_ctx = x_far * 16 + src * 2 + c
        key_block = order_ref[2 * k_ctx + r]
        parts = []
        for qi in range(2):
            live = mask_ref[order_ref[2 * q_ctx + qi], key_block]
            bias = jnp.where(live > 0, 0.0, NEG).astype(jnp.float32)
            parts.append(jnp.full((1, BLK), bias, jnp.float32))
        return jnp.concatenate(parts, axis=1)

    def attend(h, r, group):
        first = r == 0 and group == 0
        srcs = [(z + NZ + sign * dist) % NZ for dist, sign in GROUPS[group]]

        def body(slot, carry):
            q = jnp.concatenate([qall[slot, 0, h], qall[slot, 1, h]], axis=0)
            keys = jnp.concatenate([kv[src, h, r, 0] for src in srcs], axis=0)
            raw = lax.dot_general(
                keys, q, (((1,), (1,)), ((), ())), preferred_element_type=jnp.float32
            )
            blocks = [raw[i * BLK : (i + 1) * BLK] for i in range(len(srcs))]
            biases = [bias_row(slot, src, r) for src in srcs]
            tops = [
                jnp.max(b.reshape(BLK // 8, 8, ROWS), axis=0) * SCALE2 + bias
                for b, bias in zip(blocks, biases)
            ]
            top = jnp.max(functools.reduce(jnp.maximum, tops), axis=0, keepdims=True)
            before = jnp.full((1, ROWS), LOW, jnp.float32) if first else m_s[h, slot, 0:1]
            top = jnp.maximum(before, top)
            weights = [
                jnp.exp2(b * SCALE2 - (top - bias)) for b, bias in zip(blocks, biases)
            ]
            total = functools.reduce(
                jnp.add, [jnp.sum(w.reshape(BLK // 8, 8, ROWS), axis=0) for w in weights]
            )
            rounded = jnp.concatenate([w.astype(jnp.bfloat16) for w in weights], axis=0)
            values = jnp.concatenate([kv[src, h, r, 1] for src in srcs], axis=1)
            mixed = jnp.dot(values, rounded, preferred_element_type=jnp.float32)
            if not first:
                factor = jnp.exp2(before - top)
                total = total + l_s[h, slot] * factor
                mixed = mixed + o_s[h, slot] * factor
            m_s[h, slot, 0:1] = top
            l_s[h, slot] = total
            o_s[h, slot] = mixed
            return carry

        lax.fori_loop(0, 4, body, 0, unroll=1)

    def stats(h, slot):
        return m_s[h, slot, 0:1], jnp.sum(l_s[h, slot], axis=0, keepdims=True), o_s[h, slot]

    def merge(a, b):
        top = jnp.maximum(a[0], b[0])
        fa, fb = jnp.exp2(a[0] - top), jnp.exp2(b[0] - top)
        return top, a[1] * fa + b[1] * fb, a[2] * fa + b[2].astype(jnp.float32) * fb

    def share(h):
        for i, slot in enumerate((core_slot, far_core_slot)):
            top, total, mixed = stats(h, slot)
            s1[h, i, 0:1] = top
            s1[h, i, 1:2] = total
            o1[h, i] = mixed.astype(jnp.bfloat16)
        send(s1.at[h], s1r.at[h], cs.at[0], cr.at[h, 0], d_core)
        send(o1.at[h], o1r.at[h], cs.at[1], cr.at[h, 1], d_core)

    def mid(h):
        arrived(s1r.at[h], cr.at[h, 0])
        arrived(o1r.at[h], cr.at[h, 1])
        top, total, mixed = merge(
            stats(h, far_slot), (s1r[h, 1, 0:1], s1r[h, 1, 1:2], o1r[h, 1])
        )
        s2[h, 0:1] = top
        s2[h, 1:2] = total
        o2[h] = mixed.astype(jnp.bfloat16)
        send(s2.at[h], s2r.at[h], cs.at[2], cr.at[h, 2], d_far)
        send(o2.at[h], o2r.at[h], cs.at[3], cr.at[h, 3], d_far)
        top, total, mixed = merge(
            stats(h, me_slot), (s1r[h, 0, 0:1], s1r[h, 0, 1:2], o1r[h, 0])
        )
        m_s[h, me_slot, 0:1] = top
        m_s[h, me_slot, 1:2] = total
        o_s[h, me_slot] = mixed

    def fin(h):
        arrived(s2r.at[h], cr.at[h, 2])
        arrived(o2r.at[h], cr.at[h, 3])
        _, total, mixed = merge(
            (m_s[h, me_slot, 0:1], m_s[h, me_slot, 1:2], o_s[h, me_slot]),
            (s2r[h, 0:1], s2r[h, 1:2], o2r[h]),
        )
        asend[h] = jnp.transpose(mixed / total).astype(jnp.bfloat16)
        send(asend.at[h], att.at[h, hd], as_, axr.at[h, 0], d_xp)
        send(asend.at[h], att.at[h, hd], as_, axr.at[h, 1], d_xm)

    def g1(h):
        x_arrived(att_at(h), axr.at[h])
        y_first(att_at(h), as_, ayr.at[h])

    def g2(h):
        y_second(att_at(h), as_, ayr.at[h])

    def out_part(h, yy, first=False):
        rows = slice(h * HD, (h + 1) * HD)
        left = jnp.concatenate([att[h, yy], att[h, 4 + yy]], axis=1)
        right = jnp.concatenate([wo[yy, rows, :], wo[4 + yy, rows, :]], axis=0)
        part = jnp.dot(left, right, preferred_element_type=jnp.float32)
        out_acc[...] = part if first else out_acc[...] + part

    def g3(h):
        out_part(h, y, h == 0)
        out_part(h, ym)
        out_part(h, yp)
        y_last(att_at(h), ayr.at[h])
        out_part(h, y2)

    for r in range(2):
        src = tok_in.at[pl.ds(r * HALF, HALF), :]
        send(src, tok.at[r, hd], xs, xr.at[r, 0], d_xp)
        send(src, tok.at[r, hd], xs, xr.at[r, 1], d_xm)
    x_arrived(tok_at(0), xr.at[0])
    y_first(tok_at(0), ys, yr.at[0])
    for load in loads:
        load.wait()
    project(0, y, True)
    y_second(tok_at(0), ys, yr.at[0])
    x_arrived(tok_at(1), xr.at[1])
    y_first(tok_at(1), ys, yr.at[1])
    project(0, ym)
    project(0, yp)
    y_last(tok_at(0), yr.at[0])
    finish(0)
    project(1, y, True)
    y_second(tok_at(1), ys, yr.at[1])
    z_round(1)
    project(1, ym)
    project(1, yp)
    y_last(tok_at(1), yr.at[1])
    z_round(2)
    finish(1)
    out_weights()
    q_relay(0)
    z_round(3)
    q_relay(1)
    q_arrived()
    attend(0, 0, 0)
    attend(1, 0, 0)
    z_round(4)
    attend(2, 0, 0)
    attend(0, 0, 1)
    z_round(5)
    attend(1, 0, 1)
    attend(2, 0, 1)
    attend(0, 1, 0)
    z_round(6)
    attend(0, 1, 1)
    share(0)
    attend(1, 1, 0)
    z_round(7)
    mid(0)
    attend(1, 1, 1)
    share(1)
    z_round(8)
    out_weights_relay()
    attend(2, 1, 0)
    mid(1)
    fin(0)
    attend(2, 1, 1)
    share(2)
    out_weights_arrived()
    mid(2)
    fin(1)
    g1(0)
    fin(2)
    g1(1)
    g2(0)
    g1(2)
    g2(1)
    g3(0)
    g2(2)
    g3(1)
    g3(2)
    out_ref[...] = out_acc[...].astype(jnp.bfloat16)

    sent(tok.at[0, 0:4], xs)
    sent(tok.at[:, 0:6], ys)
    sent(kv.at[0:7], zs)
    sent(tok.at[0, 0:6], qs)
    sent(s1, cs.at[0])
    sent(o1, cs.at[1])
    sent(s2, cs.at[2])
    sent(o2, cs.at[3])
    sent(att, as_)
    sent(wo.at[0:7], ws)


def per_device(tokens, block_order, block_mask, w_query, w_key, w_value, w_out):
    bf, f32 = jnp.bfloat16, jnp.float32
    sem = pltpu.SemaphoreType.DMA
    smem = pl.BlockSpec(memory_space=pltpu.SMEM)
    vmem = pl.BlockSpec(memory_space=pltpu.VMEM)
    anywhere = pl.BlockSpec(memory_space=pl.ANY)
    return pl.pallas_call(
        kernel,
        out_shape=jax.ShapeDtypeStruct((ROWS, COLS), bf),
        in_specs=[smem, smem, vmem, anywhere, anywhere, anywhere, anywhere],
        out_specs=vmem,
        scratch_shapes=[
            pltpu.VMEM((2, 8, HALF, COLS), bf),
            pltpu.VMEM((3, 3072, COLS), bf),
            pltpu.VMEM((8, COLS, COLS), bf),
            pltpu.VMEM((2, HEADS, HALF, 3 * HD), f32),
            pltpu.VMEM((4, 2, HEADS, HALF, HD), bf),
            pltpu.VMEM((NZ, HEADS, 2, 2, HALF, HD), bf),
            pltpu.VMEM((HEADS, 4, 8, ROWS), f32),
            pltpu.VMEM((HEADS, 4, 8, ROWS), f32),
            pltpu.VMEM((HEADS, 4, HD, ROWS), f32),
            pltpu.VMEM((HEADS, 2, HD, ROWS), bf),
            pltpu.VMEM((HEADS, 2, 8, ROWS), f32),
            pltpu.VMEM((HEADS, 2, HD, ROWS), bf),
            pltpu.VMEM((HEADS, 2, 8, ROWS), f32),
            pltpu.VMEM((HEADS, HD, ROWS), bf),
            pltpu.VMEM((HEADS, 8, ROWS), f32),
            pltpu.VMEM((HEADS, HD, ROWS), bf),
            pltpu.VMEM((HEADS, 8, ROWS), f32),
            pltpu.VMEM((HEADS, ROWS, HD), bf),
            pltpu.VMEM((HEADS, 8, ROWS, HD), bf),
            pltpu.VMEM((ROWS, COLS), f32),
            sem((4,)),
            sem, sem((2, 2)),
            sem, sem((2, 6)),
            sem, sem((2, 4, HEADS, 2)),
            sem, sem((2, 3)),
            sem((4,)), sem((HEADS, 4)),
            sem, sem((HEADS, 2)), sem((HEADS, 6)),
            sem, sem((14,)),
        ],
        compiler_params=pltpu.CompilerParams(
            collective_id=0, has_side_effects=True, vmem_limit_bytes=60 * 1024 * 1024
        ),
    )(block_order, block_mask, tokens, w_query, w_key, w_value, w_out)


def solution(mesh):
    in_specs = (
        P("ctx", "head"),
        P(),
        P(),
        P(None, "head"),
        P(None, "head"),
        P(None, "head"),
        P("head", None),
    )
    return jax.shard_map(
        per_device, mesh=mesh, in_specs=in_specs, out_specs=P("ctx", "head"), check_vma=False
    )
```

time: 658 us -> 95.1 us (0.14)
  waiting for transfers between devices: 279 us -> 0 us
  matrix products: 162 us -> 0 us
  loops' own time: 127 us -> 0 us
  Pallas kernels: 0 us -> 92.1 us
  local copies, waits for them, and re-layouts: 61.4 us -> 1.62 us
  between operations: 13.3 us -> 0.01 us
  other arithmetic: 8.91 us -> 0 us
    all_gather x3 -> x0, waiting for transfers between devices: 201 us -> none  [the longest x1 71.3 us: per_device(): key_part = lax.all_gather(key_rows, 'ctx', axis=0, tiled=True)]
    dot_general x135 -> x0, matrix products: 162 us -> none  [the longest x64 77.5 us: update(): jnp.einsum('hqk,khd->hqd', weights.astype(jnp.bfloat16), value_tile, pref...]
    another operation x1 -> x0, loops' own time: 127 us -> none  [per_device(): lax.scan(advance, carry, (key_tiles, value_tiles, jnp.arange(tile_count,...]
    pallas_call x0 -> x1, Pallas kernels: none -> 92.1 us  [per_device(): pl.pallas_call(kernel, out_shape=jax.ShapeDtypeStruct((ROWS, COLS), bf),...]
    unnamed x5 -> x0, waiting for transfers between devices: 78 us -> none
    dynamic_slice x64 -> x0, local copies, waits for them, and re-layouts: 37.5 us -> none  [per_device(): lax.scan(advance, carry, (key_tiles, value_tiles, jnp.arange(tile_count,...]
    all_gather x2 -> x0, local copies, waits for them, and re-layouts: 17.2 us -> none  [the longest x1 8.61 us: per_device(): value_part = lax.all_gather(value_rows, 'ctx', axis=0, tiled=True)]
  transfers between devices with their start and end apart: 4 -> 0, of which waited for: 4 -> 0; matrix products, arithmetic and copies ran while one was open for 3% -> 0% of each run, Pallas kernels for 0% -> 0%
where the time goes in v2:
time: 95.1 us; the launch traced here: 93.7 us
  Pallas kernels  92.1 us (97%)
  local copies, waits for them, and re-layouts  1.62 us (2%)
    pallas_call x1, Pallas kernels, per_device(): pl.pallas_call(kernel, out_shape=jax.ShapeDtypeStruct((ROWS, COLS), bf),...  92.1 us

profile of v2, /device:TPU:8, one launch (start us, length us, event | category | flops | bytes accessed | tf_op | source)
XLA Modules:
  0.0 93.7 jit_solution(4205918526662625013)
XLA Ops:
  0.0 92.1 %shard_map.73 = bf16[256,384]{1,0:T(8,128)(2,1)} custom-call(s32[64]{0:T(128)} %order_ref.1, s32[64,64]{1,0:T(8,128)} %mask_ref.1, bf16[256,384]{1,0:T(8,128)(2,1)} %tok_in.1, bf16[3072,384]{1,0:T(8,128)(2,1)} %wq_hbm.1, bf16[3072,384]{1,0:T(8,128)(2,1)} %wk_hbm.1, bf16[3072,384]{1,0:T(8,128)(2,1)} %wv_hbm.1, bf16[384,3072]{1,0:T(8,128)(2,1)} %wo_hbm.1), custom_call_target="tpu_custom_call" | custom-call | tf_op jit(solution)/shard_map/pallas_call | solution.py:428
  92.1 1.6 %copy.9 = bf16[256,384]{1,0:T(8,128)(2,1)} copy(bf16[256,384]{1,0:T(8,128)(2,1)} %shard_map.73) | data formatting | bytes 393216
